TPU v7x, 512 devices: a whole 4x8x8 slice. The times are simulated.
512 devices in a mesh: dom: 256 (over x_hi, y, z, core), band: 2 (over x_lo).
Axes of the slice: x: 4 (x_hi: 2, x_lo: 2; x = x_hi * 2 + x_lo), y: 8, z: 8, core: 2. Of those that a mesh axis runs over, the one named last changes fastest.
Arguments:
- orbitals: float32 [256, 16, 12, 16, 128], P('dom', 'band'), may hold values from -6 to 6
- potential: float32 [256, 12, 16, 128], P('dom'), may hold values from -12 to 4
- projectors: bfloat16 [65536, 4, 128], P('dom'), may hold values from -0.359375 to 0.359375
- entry_atom: int32 [65536], P('dom'), may hold values from 0 to 1023, as said below
- entry_block: int32 [65536], P('dom'), may hold values from 0 to 191
- kb_energy: float32 [1024, 4], replicated, may hold values from 1 to 10
- panel: bfloat16 [16, 16], replicated, may hold values from -1.5 to 1.5
Outputs:
- rotated: float32 [256, 16, 12, 16, 128], P('dom', 'band')
Inputs may be any that keep to these rules, and one draw needn't show every extreme that they name: `entry_atom`: atom a is owned by domain a // 4; every entry of domain d belongs to an atom owned by d or by a domain that shares a face with d in the 8 x 8 x 4 arrangement of domains (no wrap-around).
All inputs are finite; a program needn't handle non-finite values.
Results may differ from a plain program's by a relative error of at most 0.00115.
The roundings to bfloat16 on the way count: a program that leaves them out, or rounds other values in their place, can miss the bound.
Values may be sent and summed in bfloat16 or wider, within the bound.
A program may use at most 64 MiB of HBM per device.

v0:
```python
import jax
import jax.numpy as jnp
from jax import lax
from jax.sharding import PartitionSpec as P

RADIUS = 6


COEFFS = (
    -5369.0 / 1800.0,
    12.0 / 7.0,
    -15.0 / 56.0,
    10.0 / 189.0,
    -1.0 / 112.0,
    2.0 / 1925.0,
    -1.0 / 16632.0,
)
KINETIC = -3.125
CENTER = 36.0
HALF_WIDTH = 34.0


def from_behind(block, axis, distance):
    devices = range(lax.axis_size(axis))
    route = [(i - distance, i) for i in devices if i - distance in devices]
    return lax.ppermute(block, axis, route)


def extend(values, depth_cells, position, stride, location, extent):
    length = values.shape[position]
    top_layers = lax.slice_in_dim(values, length - depth_cells, length, axis=position)
    bottom_layers = lax.slice_in_dim(values, 0, depth_cells, axis=position)
    from_lower = from_behind(top_layers, "dom", stride)
    from_upper = from_behind(bottom_layers, "dom", -stride)
    from_lower = jnp.where(location > 0, from_lower, jnp.zeros_like(from_lower))
    from_upper = jnp.where(location < extent - 1, from_upper, jnp.zeros_like(from_upper))
    return jnp.concatenate([from_lower, values, from_upper], axis=position)


def local_part(values, pot_local, geometry):
    laplace = 3.0 * COEFFS[0] * values
    for position, stride, location, extent in geometry:
        padded = extend(values, RADIUS, position, stride, location, extent)
        length = values.shape[position]
        for offset in range(1, RADIUS + 1):
            upward = lax.slice_in_dim(
                padded, RADIUS + offset, RADIUS + offset + length, axis=position
            )
            downward = lax.slice_in_dim(
                padded, RADIUS - offset, RADIUS - offset + length, axis=position
            )
            laplace = laplace + COEFFS[offset] * (upward + downward)
    return KINETIC * laplace + pot_local * values


def nonlocal_part(values, proj_values, block_index, one_hot, combine):
    orbit_count = values.shape[0]
    rows_view = values.reshape(orbit_count, -1, proj_values.shape[2])
    picked = jnp.take(rows_view, block_index, axis=1)
    intersections = jnp.einsum("epk,oek->epo", proj_values, picked, precision=lax.Precision.HIGHEST)
    atom_table = jnp.einsum("ea,epo->apo", one_hot, intersections, precision=lax.Precision.HIGHEST)
    scaled = combine(atom_table)
    per_entry = jnp.einsum("ea,apo->epo", one_hot, scaled, precision=lax.Precision.HIGHEST)
    additions = jnp.einsum("epk,epo->oek", proj_values, per_entry, precision=lax.Precision.HIGHEST)
    result = jnp.zeros_like(rows_view).at[:, block_index].add(additions)
    return result.reshape(values.shape)


def send_owner(piece, stride):
    return from_behind(piece, "dom", stride)


def send_back(piece, stride):
    return from_behind(piece, "dom", -stride)


def shards(orbitals, potential, projectors, entry_atom, entry_block, kb_energy, panel):
    start_values = orbitals[0]
    pot_local = potential[0]
    orbit_count = start_values.shape[0]
    dom_count = lax.axis_size("dom")
    dom_third = 4
    dom_second = min(8, dom_count // 8)
    plane_size = dom_second * dom_third
    dom_index = lax.axis_index("dom")
    geometry = (
        (1, plane_size, dom_index // plane_size, dom_count // plane_size),
        (2, dom_third, dom_index // dom_third % dom_second, dom_second),
        (3, 1, dom_index % dom_third, dom_third),
    )
    atom_total = kb_energy.shape[0]
    owned = atom_total // dom_count
    proj_values = projectors.astype(jnp.float32)
    strides = (0, plane_size, -plane_size, dom_third, -dom_third, 1, -1)
    owner_of = entry_atom // owned
    gap = owner_of - dom_index
    slot = jnp.zeros_like(entry_atom)
    for number in range(1, 7):
        slot = jnp.where(gap == strides[number], number, slot)
    column = slot * owned + entry_atom % owned
    one_hot = (column[:, None] == jnp.arange(7 * owned, dtype=jnp.int32)[None, :]).astype(
        jnp.float32
    )
    own_energy = lax.dynamic_slice_in_dim(kb_energy, dom_index * owned, owned, 0)

    def combine(atom_table):
        total = atom_table[0:owned]
        for number in range(1, 7):
            total = total + send_owner(
                atom_table[number * owned : (number + 1) * owned], strides[number]
            )
        scaled_own = own_energy[:, :, None] * total
        pieces = [scaled_own]
        for number in range(1, 7):
            pieces.append(send_back(scaled_own, strides[number]))
        return jnp.concatenate(pieces, axis=0)

    def apply_ham(current):
        return local_part(current, pot_local, geometry) + nonlocal_part(
            current, proj_values, entry_block, one_hot, combine
        )

    applied = apply_ham(start_values)
    first_step = (applied - CENTER * start_values) / HALF_WIDTH
    applied_again = apply_ham(first_step)
    second_step = 2.0 * (applied_again - CENTER * first_step) / HALF_WIDTH - start_values
    filtered = second_step.astype(jnp.bfloat16)
    band_index = lax.axis_index("band")
    own_rows = lax.dynamic_slice_in_dim(panel, band_index * orbit_count, orbit_count, 0)
    rotated = lax.psum_scatter(
        jnp.einsum("iabc,ij->jabc", filtered, own_rows, preferred_element_type=jnp.float32),
        "band",
        scatter_dimension=0,
        tiled=True,
    )
    return rotated[None]


def solution(mesh):
    in_specs = (
        P("dom", "band", None, None, None),
        P("dom", None, None, None),
        P("dom", None, None),
        P("dom"),
        P("dom"),
        P(),
        P(),
    )
    out_specs = P("dom", "band", None, None, None)
    return jax.shard_map(shards, mesh=mesh, in_specs=in_specs, out_specs=out_specs, check_vma=False)
```

profile of v0, /device:TPU:1, one launch (start us, length us, event | category | flops | bytes accessed | tf_op | source)
XLA Modules:
  0.0 358.8 jit_solution(11494599094950884415)
XLA Ops:
  12.8 5.4 %collective-permute-start.10 = (f32[4,4,8]{0,2,1:T(8,128)}, f32[4,4,8]{0,2,1:T(8,128)}, u32[]{:S(2)}, u32[]{:S(2)}) collective-permute-start(f32[4,4,8]{0,2,1:T(8,128)} %get-tuple-element.28), channel_id=1, source_target_pairs={{0,2},{2,4},{4,6},{6,8},{8,10},{10,12},{12,14},{14,16},{16,18},{18... | collective-permute-start | bytes 1544 | tf_op jit(solution)/shard_map/ppermute | solution.py:26
  18.2 5.3 %collective-permute-start.11 = (f32[4,4,8]{0,2,1:T(8,128)}, f32[4,4,8]{0,2,1:T(8,128)}, u32[]{:S(2)}, u32[]{:S(2)}) collective-permute-start(f32[4,4,8]{0,2,1:T(8,128)} %get-tuple-element.27), channel_id=1, source_target_pairs={{2,0},{4,2},{6,4},{8,6},{10,8},{12,10},{14,12},{16,14},{18,16},{20... | collective-permute-start | bytes 1544 | tf_op jit(solution)/shard_map/ppermute | solution.py:26
  26.6 6.0 %collective-permute-start.8 = (f32[4,4,8]{0,2,1:T(8,128)}, f32[4,4,8]{0,2,1:T(8,128)}, u32[]{:S(2)}, u32[]{:S(2)}) collective-permute-start(f32[4,4,8]{0,2,1:T(8,128)} %get-tuple-element.30), channel_id=1, source_target_pairs={{0,8},{2,10},{4,12},{6,14},{8,16},{10,18},{12,20},{14,22},{16,24},... | collective-permute-start | bytes 1544 | tf_op jit(solution)/shard_map/ppermute | solution.py:26
  38.5 3.7 %collective-permute-done.9 = f32[4,4,8]{0,2,1:T(8,128)} collective-permute-done((f32[4,4,8]{0,2,1:T(8,128)S(1)}, f32[4,4,8]{0,2,1:T(8,128)}, u32[]{:S(2)}, u32[]{:S(2)}) %collective-permute-start.9) | collective-permute-done | bytes 544 | tf_op jit(solution)/shard_map/ppermute | solution.py:26
  47.1 6.1 %collective-permute-start.13 = (f32[4,4,8]{0,2,1:T(8,128)S(1)}, f32[4,4,8]{0,2,1:T(8,128)S(1)}, u32[]{:S(2)}, u32[]{:S(2)}) collective-permute-start(f32[4,4,8]{0,2,1:T(8,128)S(1)} %fusion.199), channel_id=1, source_target_pairs={{0,64},{2,66},{4,68},{6,70},{8,72},{10,74},{12,76},{14,78},{16,80}... | collective-permute-start | bytes 1544 | tf_op jit(solution)/shard_map/ppermute | solution.py:26
  54.5 6.1 %collective-permute-start.15 = (f32[4,4,8]{0,2,1:T(8,128)S(1)}, f32[4,4,8]{0,2,1:T(8,128)S(1)}, u32[]{:S(2)}, u32[]{:S(2)}) collective-permute-start(f32[4,4,8]{0,2,1:T(8,128)S(1)} %fusion.199), channel_id=1, source_target_pairs={{0,8},{2,10},{4,12},{6,14},{8,16},{10,18},{12,20},{14,22},{16,24},... | collective-permute-start | bytes 1544 | tf_op jit(solution)/shard_map/ppermute | solution.py:26
  60.6 6.0 %collective-permute-start.16 = (f32[4,4,8]{0,2,1:T(8,128)S(1)}, f32[4,4,8]{0,2,1:T(8,128)S(1)}, u32[]{:S(2)}, u32[]{:S(2)}) collective-permute-start(f32[4,4,8]{0,2,1:T(8,128)S(1)} %fusion.199), channel_id=1, source_target_pairs={{2,0},{4,2},{6,4},{8,6},{10,8},{12,10},{14,12},{16,14},{18,16},{20... | collective-permute-start | bytes 1544 | tf_op jit(solution)/shard_map/ppermute | solution.py:26
  68.6 6.5 %collective-permute-start.3 = (f32[8,12,6,128]{3,0,2,1:T(8,128)}, f32[8,12,6,128]{3,0,2,1:T(8,128)}, u32[]{:S(2)}, u32[]{:S(2)}) collective-permute-start(f32[8,12,6,128]{3,0,2,1:T(8,128)} %copy.83), channel_id=1, source_target_pairs={{0,8},{2,10},{4,12},{6,14},{8,16},{10,18},{12,20},{14,22},{16,24},... | collective-permute-start | bytes 884744 | tf_op jit(solution)/shard_map/ppermute | solution.py:26
  76.4 2.7 collective-permute-start.4
  79.1 2.9 collective-permute-start.5
  82.0 9.7 %collective-permute-start.1 = (f32[8,6,16,128]{3,2,1,0:T(8,128)}, f32[8,6,16,128]{3,2,1,0:T(8,128)S(1)}, u32[]{:S(2)}, u32[]{:S(2)}) collective-permute-start(f32[8,6,16,128]{3,2,1,0:T(8,128)} %get-tuple-element.15), channel_id=1, source_target_pairs={{0,64},{2,66},{4,68},{6,70},{8,72},{10,74},{12,76},{14,78},{16,80}... | collective-permute-start | bytes 1179656 | tf_op jit(solution)/shard_map/ppermute | solution.py:26
  94.5 18.2 %scatter_fusion = f32[8,192,128]{2,0,1:T(8,128)S(1)} fusion(f32[8,192,128]{2,0,1:T(8,128)S(1)} %broadcast.87.clone, s32[256]{0:T(256)S(1)} %compare_select_fusion, f32[256,8,128]{2,1,0:T(8,128)} %fusion.222), kind=kCustom, calls=%fused_computation.2 | custom fusion | flops 262144 | bytes 3146752 | tf_op jit(solution)/shard_map/scatter-add | solution.py:65
  123.6 11.4 %collective-permute-done = f32[8,6,16,128]{3,2,1,0:T(8,128)} collective-permute-done((f32[8,6,16,128]{3,2,1,0:T(8,128)S(1)}, f32[8,6,16,128]{3,2,1,0:T(8,128)}, u32[]{:S(2)}, u32[]{:S(2)}) %collective-permute-start) | collective-permute-done | bytes 393248 | tf_op jit(solution)/shard_map/ppermute | solution.py:26
  136.8 11.2 %broadcast_multiply_fusion = (f32[8,12,16,128]{3,2,1,0:T(8,128)S(1)}, f32[8,12,16,128]{3,2,1,0:T(8,128)S(1)}) fusion(f32[8,12,16,128]{3,2,1,0:T(8,128)S(1)} %bitcast.53, f32[8,12,16,128]{3,0,2,1:T(8,128)S(1)} %bitcast.55, f32[12,16,128]{2,1,0:T(8,128)S(1)} %bitcast.59, f32[8,12,16,6]{3,2,1,0:T(8,128)} %copy.88, f32[8,12,16,6]{3,2,1,0:T(8,128)} %copy.86, ...), kind=kLoop, calls=%fused_computation.333 | loop fusion | flops 19267584 | bytes 4694016 | tf_op jit(solution)/shard_map/div | solution.py:124
  154.7 5.5 %collective-permute-start.24 = (f32[4,4,8]{0,2,1:T(8,128)S(1)}, f32[4,4,8]{0,2,1:T(8,128)S(1)}, u32[]{:S(2)}, u32[]{:S(2)}) collective-permute-start(f32[4,4,8]{0,2,1:T(8,128)S(1)} %get-tuple-element.20), channel_id=1, source_target_pairs={{0,64},{2,66},{4,68},{6,70},{8,72},{10,74},{12,76},{14,78},{16,80}... | collective-permute-start | bytes 1544 | tf_op jit(solution)/shard_map/ppermute | solution.py:26
  164.2 6.7 %collective-permute-start.28 = (f32[4,4,8]{0,2,1:T(8,128)S(1)}, f32[4,4,8]{0,2,1:T(8,128)S(1)}, u32[]{:S(2)}, u32[]{:S(2)}) collective-permute-start(f32[4,4,8]{0,2,1:T(8,128)S(1)} %get-tuple-element.22), channel_id=1, source_target_pairs={{0,2},{2,4},{4,6},{6,8},{8,10},{10,12},{12,14},{14,16},{16,18},{18... | collective-permute-start | bytes 1544 | tf_op jit(solution)/shard_map/ppermute | solution.py:26
  178.2 14.5 %collective-permute-start.31 = (f32[4,4,8]{0,2,1:T(8,128)S(1)}, f32[4,4,8]{0,2,1:T(8,128)S(1)}, u32[]{:S(2)}, u32[]{:S(2)}) collective-permute-start(f32[4,4,8]{0,2,1:T(8,128)S(1)} %fusion.193), channel_id=1, source_target_pairs={{0,64},{2,66},{4,68},{6,70},{8,72},{10,74},{12,76},{14,78},{16,80}... | collective-permute-start | bytes 1544 | tf_op jit(solution)/shard_map/ppermute | solution.py:26
  194.8 4.9 %collective-permute-start.33 = (f32[4,4,8]{0,2,1:T(8,128)S(1)}, f32[4,4,8]{0,2,1:T(8,128)S(1)}, u32[]{:S(2)}, u32[]{:S(2)}) collective-permute-start(f32[4,4,8]{0,2,1:T(8,128)S(1)} %fusion.193), channel_id=1, source_target_pairs={{0,8},{2,10},{4,12},{6,14},{8,16},{10,18},{12,20},{14,22},{16,24},... | collective-permute-start | bytes 1544 | tf_op jit(solution)/shard_map/ppermute | solution.py:26
  202.3 5.1 %collective-permute-start.34 = (f32[4,4,8]{0,2,1:T(8,128)S(1)}, f32[4,4,8]{0,2,1:T(8,128)S(1)}, u32[]{:S(2)}, u32[]{:S(2)}) collective-permute-start(f32[4,4,8]{0,2,1:T(8,128)S(1)} %fusion.193), channel_id=1, source_target_pairs={{2,0},{4,2},{6,4},{8,6},{10,8},{12,10},{14,12},{16,14},{18,16},{20... | collective-permute-start | bytes 1544 | tf_op jit(solution)/shard_map/ppermute | solution.py:26
  216.3 3.1 collective-permute-start.22
  219.4 20.2 %collective-permute-start.19 = (f32[8,6,16,128]{3,2,1,0:T(8,128)}, f32[8,6,16,128]{3,2,1,0:T(8,128)}, u32[]{:S(2)}, u32[]{:S(2)}) collective-permute-start(f32[8,6,16,128]{3,2,1,0:T(8,128)} %get-tuple-element.9), channel_id=1, source_target_pairs={{0,64},{2,66},{4,68},{6,70},{8,72},{10,74},{12,76},{14,78},{16,80}... | collective-permute-start | bytes 1179656 | tf_op jit(solution)/shard_map/ppermute | solution.py:26
  242.4 18.2 %scatter_fusion.1 = f32[8,192,128]{2,0,1:T(8,128)S(1)} fusion(f32[8,192,128]{2,0,1:T(8,128)S(1)} %broadcast.87, s32[256]{0:T(256)S(1)} %compare_select_fusion, f32[256,8,128]{2,1,0:T(8,128)} %fusion.223), kind=kCustom, calls=%fused_computation.3 | custom fusion | flops 262144 | bytes 3146752 | tf_op jit(solution)/shard_map/scatter-add | solution.py:65
  276.7 12.4 %subtract_convert_fusion = bf16[8,12,16,128]{3,2,1,0:T(8,128)(2,1)} fusion(f32[8,12,16,128]{3,2,1,0:T(8,128)S(1)} %get-tuple-element.7, f32[8,12,16,128]{3,0,2,1:T(8,128)S(1)} %bitcast.54, f32[8,12,16,128]{3,2,1,0:T(8,128)S(1)} %get-tuple-element.6, f32[8,12,16,6]{3,2,1,0:T(8,128)} %copy.100, f32[8,12,16,6]{3,2,1,0:T(8,128)} %copy.98, ...), kind=kLoop, calls=%fused_computation.322 | loop fusion | flops 19660800 | bytes 5087232 | tf_op jit(solution)/shard_map/convert_element_type | solution.py:127
  291.7 58.0 %reduce-scatter.2.cloned.1.call-done = f32[8,12,16,128]{3,0,2,1:T(8,128)} async-done(((f32[16,12,16,128]{3,0,2,1:T(8,128)}), f32[8,12,16,128]{3,0,2,1:T(8,128)}) %reduce-scatter.2.cloned.1.call-update) | async-done | bytes 786448 | tf_op jit(solution)/shard_map/reduce_scatter | solution.py:130
  (137 shorter events, 95.0 us)
Async XLA Ops:
  6.5 343.2 %reduce-scatter.2.cloned.1.call-start = ((), (), s32[]{:S(2)}) async-start(), calls=%async_computation.1 | async-start | bytes 2359296 | tf_op jit(solution)/shard_map/reduce_scatter | solution.py:130
  12.8 22.6 %collective-permute-start.10 = (f32[4,4,8]{0,2,1:T(8,128)}, f32[4,4,8]{0,2,1:T(8,128)}, u32[]{:S(2)}, u32[]{:S(2)}) collective-permute-start(f32[4,4,8]{0,2,1:T(8,128)} %get-tuple-element.28), channel_id=1, source_target_pairs={{0,2},{2,4},{4,6},{6,8},{8,10},{10,12},{12,14},{14,16},{16,18},{18... | collective-permute-start | bytes 1544 | tf_op jit(solution)/shard_map/ppermute | solution.py:26
  18.2 20.3 %collective-permute-start.11 = (f32[4,4,8]{0,2,1:T(8,128)}, f32[4,4,8]{0,2,1:T(8,128)}, u32[]{:S(2)}, u32[]{:S(2)}) collective-permute-start(f32[4,4,8]{0,2,1:T(8,128)} %get-tuple-element.27), channel_id=1, source_target_pairs={{2,0},{4,2},{6,4},{8,6},{10,8},{12,10},{14,12},{16,14},{18,16},{20... | collective-permute-start | bytes 1544 | tf_op jit(solution)/shard_map/ppermute | solution.py:26
  43.0 23.7 %collective-permute-start.12 = (f32[4,4,8]{0,2,1:T(8,128)S(1)}, f32[4,4,8]{0,2,1:T(8,128)S(1)}, u32[]{:S(2)}, u32[]{:S(2)}) collective-permute-start(f32[4,4,8]{0,2,1:T(8,128)S(1)} %fusion.199), channel_id=1, source_target_pairs={{64,0},{66,2},{68,4},{70,6},{72,8},{74,10},{76,12},{78,14},{80,16}... | collective-permute-start | bytes 1544 | tf_op jit(solution)/shard_map/ppermute | solution.py:26
  47.1 21.5 %collective-permute-start.13 = (f32[4,4,8]{0,2,1:T(8,128)S(1)}, f32[4,4,8]{0,2,1:T(8,128)S(1)}, u32[]{:S(2)}, u32[]{:S(2)}) collective-permute-start(f32[4,4,8]{0,2,1:T(8,128)S(1)} %fusion.199), channel_id=1, source_target_pairs={{0,64},{2,66},{4,68},{6,70},{8,72},{10,74},{12,76},{14,78},{16,80}... | collective-permute-start | bytes 1544 | tf_op jit(solution)/shard_map/ppermute | solution.py:26
  53.2 21.9 %collective-permute-start.14 = (f32[4,4,8]{0,2,1:T(8,128)S(1)}, f32[4,4,8]{0,2,1:T(8,128)S(1)}, u32[]{:S(2)}, u32[]{:S(2)}) collective-permute-start(f32[4,4,8]{0,2,1:T(8,128)S(1)} %fusion.199), channel_id=1, source_target_pairs={{8,0},{10,2},{12,4},{14,6},{16,8},{18,10},{20,12},{22,14},{24,16},... | collective-permute-start | bytes 1544 | tf_op jit(solution)/shard_map/ppermute | solution.py:26
  54.5 21.9 %collective-permute-start.15 = (f32[4,4,8]{0,2,1:T(8,128)S(1)}, f32[4,4,8]{0,2,1:T(8,128)S(1)}, u32[]{:S(2)}, u32[]{:S(2)}) collective-permute-start(f32[4,4,8]{0,2,1:T(8,128)S(1)} %fusion.199), channel_id=1, source_target_pairs={{0,8},{2,10},{4,12},{6,14},{8,16},{10,18},{12,20},{14,22},{16,24},... | collective-permute-start | bytes 1544 | tf_op jit(solution)/shard_map/ppermute | solution.py:26
  60.6 18.5 %collective-permute-start.16 = (f32[4,4,8]{0,2,1:T(8,128)S(1)}, f32[4,4,8]{0,2,1:T(8,128)S(1)}, u32[]{:S(2)}, u32[]{:S(2)}) collective-permute-start(f32[4,4,8]{0,2,1:T(8,128)S(1)} %fusion.199), channel_id=1, source_target_pairs={{2,0},{4,2},{6,4},{8,6},{10,8},{12,10},{14,12},{16,14},{18,16},{20... | collective-permute-start | bytes 1544 | tf_op jit(solution)/shard_map/ppermute | solution.py:26
  68.6 50.6 %collective-permute-start.3 = (f32[8,12,6,128]{3,0,2,1:T(8,128)}, f32[8,12,6,128]{3,0,2,1:T(8,128)}, u32[]{:S(2)}, u32[]{:S(2)}) collective-permute-start(f32[8,12,6,128]{3,0,2,1:T(8,128)} %copy.83), channel_id=1, source_target_pairs={{0,8},{2,10},{4,12},{6,14},{8,16},{10,18},{12,20},{14,22},{16,24},... | collective-permute-start | bytes 884744 | tf_op jit(solution)/shard_map/ppermute | solution.py:26
  75.1 45.9 %collective-permute-start.2 = (f32[8,12,6,128]{3,0,2,1:T(8,128)}, f32[8,12,6,128]{3,0,2,1:T(8,128)}, u32[]{:S(2)}, u32[]{:S(2)}) collective-permute-start(f32[8,12,6,128]{3,0,2,1:T(8,128)} %copy.81), channel_id=1, source_target_pairs={{8,0},{10,2},{12,4},{14,6},{16,8},{18,10},{20,12},{22,14},{24,16},... | collective-permute-start | bytes 884744 | tf_op jit(solution)/shard_map/ppermute | solution.py:26
  76.4 36.3 %collective-permute-start.4 = (f32[8,12,16,6]{2,0,3,1:T(8,128)}, f32[8,12,16,6]{2,0,3,1:T(8,128)}, u32[]{:S(2)}, u32[]{:S(2)}) collective-permute-start(f32[8,12,16,6]{2,0,3,1:T(8,128)} %copy.85), channel_id=1, source_target_pairs={{2,0},{4,2},{6,4},{8,6},{10,8},{12,10},{14,12},{16,14},{18,16},{20... | collective-permute-start | bytes 110600 | tf_op jit(solution)/shard_map/ppermute | solution.py:26
  79.1 36.1 %collective-permute-start.5 = (f32[8,12,16,6]{2,0,3,1:T(8,128)}, f32[8,12,16,6]{2,0,3,1:T(8,128)}, u32[]{:S(2)}, u32[]{:S(2)}) collective-permute-start(f32[8,12,16,6]{2,0,3,1:T(8,128)} %copy.87), channel_id=1, source_target_pairs={{0,2},{2,4},{4,6},{6,8},{8,10},{10,12},{12,14},{14,16},{16,18},{18... | collective-permute-start | bytes 110600 | tf_op jit(solution)/shard_map/ppermute | solution.py:26
  82.0 40.8 %collective-permute-start.1 = (f32[8,6,16,128]{3,2,1,0:T(8,128)}, f32[8,6,16,128]{3,2,1,0:T(8,128)S(1)}, u32[]{:S(2)}, u32[]{:S(2)}) collective-permute-start(f32[8,6,16,128]{3,2,1,0:T(8,128)} %get-tuple-element.15), channel_id=1, source_target_pairs={{0,64},{2,66},{4,68},{6,70},{8,72},{10,74},{12,76},{14,78},{16,80}... | collective-permute-start | bytes 1179656 | tf_op jit(solution)/shard_map/ppermute | solution.py:26
  112.7 22.3 %collective-permute-start = (f32[8,6,16,128]{3,2,1,0:T(8,128)S(1)}, f32[8,6,16,128]{3,2,1,0:T(8,128)}, u32[]{:S(2)}, u32[]{:S(2)}) collective-permute-start(f32[8,6,16,128]{3,2,1,0:T(8,128)S(1)} %copy-done.3), channel_id=1, source_target_pairs={{64,0},{66,2},{68,4},{70,6},{72,8},{74,10},{76,12},{78,14},{80,16}... | collective-permute-start | bytes 1179656 | tf_op jit(solution)/shard_map/ppermute | solution.py:26
  154.7 16.2 %collective-permute-start.24 = (f32[4,4,8]{0,2,1:T(8,128)S(1)}, f32[4,4,8]{0,2,1:T(8,128)S(1)}, u32[]{:S(2)}, u32[]{:S(2)}) collective-permute-start(f32[4,4,8]{0,2,1:T(8,128)S(1)} %get-tuple-element.20), channel_id=1, source_target_pairs={{0,64},{2,66},{4,68},{6,70},{8,72},{10,74},{12,76},{14,78},{16,80}... | collective-permute-start | bytes 1544 | tf_op jit(solution)/shard_map/ppermute | solution.py:26
  176.0 31.4 %collective-permute-start.30 = (f32[4,4,8]{0,2,1:T(8,128)S(1)}, f32[4,4,8]{0,2,1:T(8,128)S(1)}, u32[]{:S(2)}, u32[]{:S(2)}) collective-permute-start(f32[4,4,8]{0,2,1:T(8,128)S(1)} %fusion.193), channel_id=1, source_target_pairs={{64,0},{66,2},{68,4},{70,6},{72,8},{74,10},{76,12},{78,14},{80,16}... | collective-permute-start | bytes 1544 | tf_op jit(solution)/shard_map/ppermute | solution.py:26
  178.2 32.5 %collective-permute-start.31 = (f32[4,4,8]{0,2,1:T(8,128)S(1)}, f32[4,4,8]{0,2,1:T(8,128)S(1)}, u32[]{:S(2)}, u32[]{:S(2)}) collective-permute-start(f32[4,4,8]{0,2,1:T(8,128)S(1)} %fusion.193), channel_id=1, source_target_pairs={{0,64},{2,66},{4,68},{6,70},{8,72},{10,74},{12,76},{14,78},{16,80}... | collective-permute-start | bytes 1544 | tf_op jit(solution)/shard_map/ppermute | solution.py:26
  193.6 19.5 %collective-permute-start.32 = (f32[4,4,8]{0,2,1:T(8,128)S(1)}, f32[4,4,8]{0,2,1:T(8,128)S(1)}, u32[]{:S(2)}, u32[]{:S(2)}) collective-permute-start(f32[4,4,8]{0,2,1:T(8,128)S(1)} %fusion.193), channel_id=1, source_target_pairs={{8,0},{10,2},{12,4},{14,6},{16,8},{18,10},{20,12},{22,14},{24,16},... | collective-permute-start | bytes 1544 | tf_op jit(solution)/shard_map/ppermute | solution.py:26
  194.8 19.5 %collective-permute-start.33 = (f32[4,4,8]{0,2,1:T(8,128)S(1)}, f32[4,4,8]{0,2,1:T(8,128)S(1)}, u32[]{:S(2)}, u32[]{:S(2)}) collective-permute-start(f32[4,4,8]{0,2,1:T(8,128)S(1)} %fusion.193), channel_id=1, source_target_pairs={{0,8},{2,10},{4,12},{6,14},{8,16},{10,18},{12,20},{14,22},{16,24},... | collective-permute-start | bytes 1544 | tf_op jit(solution)/shard_map/ppermute | solution.py:26
  210.7 59.7 %collective-permute-start.21 = (f32[8,12,6,128]{3,0,2,1:T(8,128)}, f32[8,12,6,128]{3,0,2,1:T(8,128)}, u32[]{:S(2)}, u32[]{:S(2)}) collective-permute-start(f32[8,12,6,128]{3,0,2,1:T(8,128)} %copy.95), channel_id=1, source_target_pairs={{0,8},{2,10},{4,12},{6,14},{8,16},{10,18},{12,20},{14,22},{16,24},... | collective-permute-start | bytes 884744 | tf_op jit(solution)/shard_map/ppermute | solution.py:26
  213.1 59.2 %collective-permute-start.20 = (f32[8,12,6,128]{3,0,2,1:T(8,128)}, f32[8,12,6,128]{3,0,2,1:T(8,128)}, u32[]{:S(2)}, u32[]{:S(2)}) collective-permute-start(f32[8,12,6,128]{3,0,2,1:T(8,128)} %copy.93), channel_id=1, source_target_pairs={{8,0},{10,2},{12,4},{14,6},{16,8},{18,10},{20,12},{22,14},{24,16},... | collective-permute-start | bytes 884744 | tf_op jit(solution)/shard_map/ppermute | solution.py:26
  214.4 46.2 %collective-permute-start.23 = (f32[8,12,16,6]{2,0,3,1:T(8,128)}, f32[8,12,16,6]{2,0,3,1:T(8,128)}, u32[]{:S(2)}, u32[]{:S(2)}) collective-permute-start(f32[8,12,16,6]{2,0,3,1:T(8,128)} %copy.99), channel_id=1, source_target_pairs={{0,2},{2,4},{4,6},{6,8},{8,10},{10,12},{12,14},{14,16},{16,18},{18... | collective-permute-start | bytes 110600 | tf_op jit(solution)/shard_map/ppermute | solution.py:26
  216.3 47.5 %collective-permute-start.22 = (f32[8,12,16,6]{2,0,3,1:T(8,128)}, f32[8,12,16,6]{2,0,3,1:T(8,128)}, u32[]{:S(2)}, u32[]{:S(2)}) collective-permute-start(f32[8,12,16,6]{2,0,3,1:T(8,128)} %copy.97), channel_id=1, source_target_pairs={{2,0},{4,2},{6,4},{8,6},{10,8},{12,10},{14,12},{16,14},{18,16},{20... | collective-permute-start | bytes 110600 | tf_op jit(solution)/shard_map/ppermute | solution.py:26
  219.4 54.7 %collective-permute-start.19 = (f32[8,6,16,128]{3,2,1,0:T(8,128)}, f32[8,6,16,128]{3,2,1,0:T(8,128)}, u32[]{:S(2)}, u32[]{:S(2)}) collective-permute-start(f32[8,6,16,128]{3,2,1,0:T(8,128)} %get-tuple-element.9), channel_id=1, source_target_pairs={{0,64},{2,66},{4,68},{6,70},{8,72},{10,74},{12,76},{14,78},{16,80}... | collective-permute-start | bytes 1179656 | tf_op jit(solution)/shard_map/ppermute | solution.py:26
  (23 other events, 254.0 us)
Sparse Core Ops, SparseCore 0:
  291.9 57.8 reduce-scatter.1
where the time goes:
time: 362 us; the launch traced here: 359 us
  starting transfers between devices  146 us (40%)
  other arithmetic  80.7 us (22%)
  waiting for transfers between devices  75.4 us (21%)
  local copies, waits for them, and re-layouts  32 us (9%)
  between operations  14.1 us (4%)
  matrix products  10.9 us (3%)
    ppermute x36, starting transfers between devices, from_behind(): return lax.ppermute(block, axis, route)  146 us
    reduce_scatter x1, waiting for transfers between devices, shards(): lax.psum_scatter(jnp.einsum('iabc,ij->jabc', filtered, own_rows, preferre...  58 us
    scatter-add x2, other arithmetic, nonlocal_part(): result = jnp.zeros_like(rows_view).at[:, block_index].add(additions)  36.4 us
    ppermute x36, waiting for transfers between devices, from_behind(): return lax.ppermute(block, axis, route)  17.3 us
    convert_element_type x1, other arithmetic, shards(): filtered = second_step.astype(jnp.bfloat16)  12.4 us
    div x1, other arithmetic, shards(): first_step = (applied - CENTER * start_values) / HALF_WIDTH  11.2 us
    select_n x6, other arithmetic, extend(): jnp.where(location < extent - 1, from_upper, jnp.zeros_like(from_upper))  9.93 us
    slice x10, local copies, waits for them, and re-layouts, extend(): bottom_layers = lax.slice_in_dim(values, 0, depth_cells, axis=position)  8.33 us
  transfers between devices with their start and end apart: 37, of which 4 were waited for; matrix products, arithmetic and copies ran while one was open for 22% of the time, Pallas kernels for 0%

commit v1 on v0

v1 whole, which is shorter than its diff:
```python
import jax
import jax.numpy as jnp
import ml_dtypes
import numpy as np
from jax import lax
from jax.experimental import pallas as pl
from jax.experimental.pallas import tpu as pltpu
from jax.sharding import PartitionSpec as P

COEFFS = (
    -5369.0 / 1800.0,
    12.0 / 7.0,
    -15.0 / 56.0,
    10.0 / 189.0,
    -1.0 / 112.0,
    2.0 / 1925.0,
    -1.0 / 16632.0,
)
KINETIC = -3.125
CENTER = 36.0
HALF_WIDTH = 34.0
REACH = 6

DOM_Z = 4
DOM_Y = 8
NORB = 8
CX, CY, CZ = 12, 16, 128
ENT = 256
ROWS = CX * CY
HALF = ROWS // 2
OWNED = 4
CHUNK = 2
NCHUNK = NORB // CHUNK
GROUP = 4
NGROUP = NORB // GROUP
LANE_SLOT = 16
SCALE = 64 * 1.0937445
F32 = jnp.float32
BF16 = jnp.bfloat16
OPPOSITE = (1, 0, 3, 2, 5, 4)
NN = (((1,), (0,)), ((), ()))
NT = (((1,), (1,)), ((), ()))


def tap(distance):
    return SCALE * COEFFS[abs(distance)]


def stencil_tables():
    plane = np.zeros((ROWS, 8 * HALF), np.float32)
    for x in range(CX):
        for y in range(CY):
            row = y // 8 * HALF + x * 8 + y % 8
            for step in (s for s in range(-REACH, REACH + 1) if s):
                to = x + step
                if 0 <= to < CX:
                    near = y // 8 * HALF + to * 8 + y % 8
                    plane[row, near] += tap(step)
                    plane[row, 6 * HALF + near] += tap(step)
                else:
                    place = (to + REACH) * 8 if to < 0 else HALF // 2 + (to - CX) * 8
                    plane[row, (2 + y // 8) * HALF + place + y % 8] += tap(step)
                to = y + step
                if 0 <= to < CY:
                    near = to // 8 * HALF + x * 8 + to % 8
                    plane[row, near] += tap(step)
                    plane[row, 6 * HALF + near] += tap(step)
                elif to < 0:
                    plane[row, 4 * HALF + x * 8 + to + 8] += tap(step)
                else:
                    plane[row, 5 * HALF + x * 8 + to - CY] += tap(step)
    line = np.zeros((2 * CZ, CZ), np.float32)
    edge = np.zeros((NORB, 2 * CZ, CZ), np.float32)
    pack = np.zeros((NORB, CZ, 2 * CZ), np.float32)
    for z in range(CZ):
        for step in (s for s in range(-REACH, REACH + 1) if s):
            to = z + step
            for o in range(NORB):
                if to < 0:
                    edge[o, o * LANE_SLOT + to + REACH, z] = tap(step)
                elif to >= CZ:
                    edge[o, CZ + o * LANE_SLOT + to - CZ, z] = tap(step)
            if 0 <= to < CZ:
                line[to, z] = line[CZ + to, z] = tap(step)
    for o in range(NORB):
        for k in range(REACH):
            pack[o, k, o * LANE_SLOT + k] = 1.0
            pack[o, CZ - REACH + k, CZ + o * LANE_SLOT + k] = 1.0
    return [t.astype(ml_dtypes.bfloat16) for t in (plane, line, edge, pack)]


def dot(a, b, dims=NN):
    return lax.dot_general(a, b, dims, preferred_element_type=F32)


def iota(shape, axis):
    return lax.broadcasted_iota(jnp.int32, shape, axis)


def split(values):
    high = values.astype(BF16)
    return high, (values - high.astype(F32)).astype(BF16)


def kernel(
    orb_hbm, pot_hbm, proj_hbm, atom_ref, block_ref, energy_hbm, panel_ref, plane_hbm, line_hbm, edge_hbm, pack_hbm,
    out_hbm,
    start, field, first, weight, proj, energy, plane, line, edge, pack,
    z_out, z_in, filtered, partner, result,
    pick, spread, slots, picked, inner, additions, table_out, table_in, scaled_out, scaled_in, mix,
    local_sem, halo_send, halo_recv, table_send, table_recv, band_send, band_recv, out_sem,
):
    dom = lax.axis_index("dom")
    band = lax.axis_index("band")
    count = lax.axis_size("dom")
    plane_size = DOM_Y * DOM_Z
    at = (dom // plane_size, dom // DOM_Z % DOM_Y, dom % DOM_Z)
    extents = (count // plane_size, DOM_Y, DOM_Z)
    strides = (plane_size, -plane_size, DOM_Z, -DOM_Z, 1, -1)
    has = []
    for axis in range(3):
        has.append(at[axis] < extents[axis] - 1)
        has.append(at[axis] > 0)

    def toward(d):
        return {"dom": jnp.clip(dom + strides[d], 0, count - 1)}

    loads = []

    def load(src, dst):
        copy = pltpu.make_async_copy(src, dst, local_sem.at[len(loads)])
        copy.start()
        loads.append(copy)
        return copy

    orb_loads = [
        [
            load(
                orb_hbm.at[0, pl.ds(c * CHUNK, CHUNK), :, pl.ds(h * 8, 8), :],
                start.at[pl.ds(c * CHUNK, CHUNK), h],
            )
            for h in range(2)
        ]
        for c in range(NCHUNK)
    ]
    pack_load = load(pack_hbm, pack)
    proj_load = load(proj_hbm, proj)
    pot_loads = [load(pot_hbm.at[0, :, pl.ds(h * 8, 8), :], weight.at[h]) for h in range(2)]
    width = energy.shape[1]
    energy_load = load(energy_hbm.at[:, pl.ds(pl.multiple_of(dom * OWNED // width * width, width), width)], energy)
    plane_load = load(plane_hbm, plane)
    line_load = load(line_hbm, line)
    edge_load = load(edge_hbm, edge)

    barrier = pltpu.get_barrier_semaphore()
    partners = jnp.int32(1)
    for d in range(6):
        partners = partners + has[d].astype(jnp.int32)

        @pl.when(has[d])
        def _():
            pl.semaphore_signal(barrier, inc=1, device_id=toward(d), device_id_type=pl.DeviceIdType.MESH)

    pl.semaphore_signal(barrier, inc=1, device_id={"band": 1 - band}, device_id_type=pl.DeviceIdType.MESH)

    for h in range(2):
        for d in range(6):

            @pl.when(jnp.logical_not(has[OPPOSITE[d]]))
            def _():
                if d == 0:
                    field[h, :, 2:4, 0 : HALF // 2, :] = jnp.zeros((NORB, 2, HALF // 2, CZ), BF16)
                elif d == 1:
                    field[h, :, 2:4, HALF // 2 : HALF, :] = jnp.zeros((NORB, 2, HALF // 2, CZ), BF16)
                elif d == 2:
                    field[h, :, 4, :, :] = jnp.zeros((NORB, HALF, CZ), BF16)
                elif d == 3:
                    field[h, :, 5, :, :] = jnp.zeros((NORB, HALF, CZ), BF16)
                else:
                    z_in[h, :, d - 4] = jnp.zeros((NCHUNK, ROWS, CZ), BF16)
                table_in[h, :, d] = jnp.zeros((NGROUP, 8, CZ), F32)
                scaled_in[h, :, d] = jnp.zeros((NGROUP, 8, CZ), F32)

    table_out[...] = jnp.zeros(table_out.shape, F32)

    def halo(h, c, d):
        own = pl.ds(c * CHUNK, CHUNK)
        low, high = pl.ds(0, HALF // 2), pl.ds(HALF // 2, HALF // 2)
        if d == 0:
            src, dst = field.at[h, own, 0:2, high, :], field.at[h, own, 2:4, low, :]
        elif d == 1:
            src, dst = field.at[h, own, 0:2, low, :], field.at[h, own, 2:4, high, :]
        elif d == 2:
            src, dst = field.at[h, own, 1], field.at[h, own, 4]
        elif d == 3:
            src, dst = field.at[h, own, 0], field.at[h, own, 5]
        elif d == 4:
            src, dst = z_out.at[h, c, 1], z_in.at[h, c, 0]
        else:
            src, dst = z_out.at[h, c, 0], z_in.at[h, c, 1]
        return pltpu.make_async_remote_copy(
            src_ref=src,
            dst_ref=dst,
            send_sem=halo_send.at[h, c, d],
            recv_sem=halo_recv.at[h, c, d],
            device_id=toward(d),
            device_id_type=pl.DeviceIdType.MESH,
        )

    def table(h, g, kind, d):
        return pltpu.make_async_remote_copy(
            src_ref=(table_out, scaled_out)[kind].at[h, g],
            dst_ref=(table_in, scaled_in)[kind].at[h, g, d],
            send_sem=table_send.at[h, g, kind, d],
            recv_sem=table_recv.at[h, g, kind, d],
            device_id=toward(d),
            device_id_type=pl.DeviceIdType.MESH,
        )

    def exchange(c):
        return pltpu.make_async_remote_copy(
            src_ref=filtered.at[pl.ds(c * CHUNK, CHUNK)],
            dst_ref=partner.at[pl.ds(c * CHUNK, CHUNK)],
            send_sem=band_send.at[c],
            recv_sem=band_recv.at[c],
            device_id={"band": 1 - band},
            device_id_type=pl.DeviceIdType.MESH,
        )

    def start_all(make):
        for d in range(6):

            @pl.when(has[d])
            def _():
                make(d).start()

    def wait_recv_all(make):
        for d in range(6):

            @pl.when(has[OPPOSITE[d]])
            def _():
                make(d).wait_recv()

    def wait_send_all(make):
        for d in range(6):

            @pl.when(has[d])
            def _():
                make(d).wait_send()

    def high_of(h, o):
        return field[h, o, 0:2].reshape(ROWS, CZ)

    def low_of(h, o):
        return field[h, o, 6:8].reshape(ROWS, CZ)

    def keep(h, o, values):
        high, low = split(values.reshape(2, HALF, CZ))
        field[h, o, 0:2] = high
        field[h, o, 6:8] = low

    def send_halos(h, c):
        ends = None
        for o in range(c * CHUNK, (c + 1) * CHUNK):
            part = dot(high_of(h, o), pack[o])
            ends = part if ends is None else ends + part
        z_out[h, c, 0] = ends[:, :CZ].astype(BF16)
        z_out[h, c, 1] = ends[:, CZ:].astype(BF16)
        start_all(lambda d: halo(h, c, d))

    for c in range(NCHUNK):
        for copy in orb_loads[c]:
            copy.wait()
        for o in range(c * CHUNK, (c + 1) * CHUNK):
            keep(0, o, start[o].reshape(ROWS, CZ))
        if c == 0:
            pack_load.wait()
            pl.semaphore_wait(barrier, partners)
        send_halos(0, c)

    proj_load.wait()
    mask = iota((32, CZ), 0) == iota((32, CZ), 1) // 4
    block = block_ref[...]
    row = ((block % 16) // 8) * HALF + (block // 16) * 8 + block % 8
    one_hot = (iota((ROWS, ENT), 0) == row).astype(F32).astype(BF16)
    spread[:, :ENT] = one_hot
    spread[:, ENT:] = one_hot
    diagonal = iota((ENT, ENT), 0) == iota((ENT, ENT), 1)
    row_column = jnp.sum(jnp.where(diagonal, row.astype(F32), 0.0), axis=1, keepdims=True)
    pick[...] = (iota((ENT, ROWS), 1).astype(F32) == row_column).astype(F32).astype(BF16)
    atom = atom_ref[...]
    gap = atom // OWNED - dom
    slot = jnp.zeros_like(gap)
    for d in range(6):
        slot = jnp.where(gap == strides[d], d + 1, slot)
    code = (slot * OWNED + atom % OWNED).astype(F32)
    code_column = jnp.sum(jnp.where(diagonal, code, 0.0), axis=1, keepdims=True)
    for q in range(8):
        lanes = jnp.sum(jnp.where(mask, code_column[q * 32 : (q + 1) * 32], 0.0), axis=0, keepdims=True)
        wanted = lanes * 4.0 + (iota((1, CZ), 1) % 4).astype(F32)
        slots[:, q * CZ : (q + 1) * CZ] = (iota((CZ, CZ), 0).astype(F32) == wanted).astype(F32).astype(BF16)

    energy_load.wait()
    here = dom * OWNED % width + iota((width, CZ), 1) // 4
    chosen = jnp.logical_and(iota((width, CZ), 0) == here, iota((width, CZ), 1) < 4 * OWNED)
    chosen = chosen.astype(F32).astype(BF16)
    high, low = split(energy[...])
    levels = dot(high, chosen) + dot(low, chosen)
    levels = jnp.where(iota((4, CZ), 1) % 4 == iota((4, CZ), 0), levels, 0.0)
    own_energy = jnp.sum(levels, axis=0, keepdims=True) * (SCALE / KINETIC)

    def project(h, g):
        for i in range(GROUP):
            o = g * GROUP + i
            both = jnp.concatenate([high_of(h, o), low_of(h, o)], axis=1)
            picked[:, i] = dot(pick[...], both).astype(BF16).reshape(8, 32, 2 * CZ)
        for q in range(8):
            values = proj[q * CZ : (q + 1) * CZ, :]
            pairs = dot(picked[q].reshape(GROUP * 32, 2 * CZ), jnp.concatenate([values, values], axis=1), NT)
            kept = jnp.where(mask.reshape(1, 4, 8, CZ), pairs.reshape(GROUP, 4, 8, CZ), 0.0)
            inner[:, q * CZ : (q + 1) * CZ] = jnp.sum(kept, axis=1).reshape(GROUP * 8, CZ)
        high, low = split(inner[...])
        sums = dot(jnp.concatenate([high, low], axis=0), slots[...], NT).reshape(2, GROUP, 8, CZ)
        table_out[h, g, 0:GROUP] = jnp.sum(jnp.sum(sums, axis=0), axis=1)
        start_all(lambda d: table(h, g, 0, d))

    def scale_sums(h, g):
        wait_recv_all(lambda d: table(h, g, 0, d))
        total = table_out[h, g]
        for d in range(6):
            total = total + pltpu.roll(table_in[h, g, d], CZ - LANE_SLOT * (d + 1), 1)
        scaled_out[h, g] = jnp.where(iota((8, CZ), 1) < LANE_SLOT, total * own_energy, 0.0)
        start_all(lambda d: table(h, g, 1, d))

    def add_projectors(h, g):
        wait_recv_all(lambda d: table(h, g, 1, d))
        scaled = scaled_out[h, g]
        for d in range(6):
            scaled = scaled + pltpu.roll(scaled_in[h, g, d], LANE_SLOT * (OPPOSITE[d] + 1), 1)
        high, low = split(scaled)
        entries = dot(jnp.concatenate([high, low], axis=0), slots[...])
        for q in range(8):
            lanes = slice(q * CZ, (q + 1) * CZ)
            rows = []
            for i in range(GROUP):
                rows.append(
                    jnp.concatenate(
                        [
                            jnp.where(mask, entries[i : i + 1, lanes], 0.0).astype(BF16),
                            jnp.where(mask, entries[8 + i : 9 + i, lanes], 0.0).astype(BF16),
                        ],
                        axis=1,
                    )
                )
            values = proj[lanes, :]
            added = dot(jnp.concatenate(rows, axis=0), jnp.concatenate([values, values], axis=0))
            high, low = split(added.reshape(GROUP, 32, CZ))
            additions[g * GROUP : (g + 1) * GROUP, 0, q * 32 : (q + 1) * 32] = high
            additions[g * GROUP : (g + 1) * GROUP, 1, q * 32 : (q + 1) * 32] = low

    def applied(h, c, o):
        total = dot(plane[...], field[h, o].reshape(8 * HALF, CZ))
        total = total + dot(jnp.concatenate([high_of(h, o), low_of(h, o)], axis=1), line[...])
        total = total + dot(jnp.concatenate([z_in[h, c, 0], z_in[h, c, 1]], axis=1), edge[o])
        return total + dot(spread[...], additions[o].reshape(2 * ENT, CZ))

    for g in range(NGROUP):
        project(0, g)

    jj = iota((CZ, 16), 0) // 16 + band * NORB
    choose_out = (iota((CZ, 16), 1) == jj).astype(F32).astype(BF16)
    column = iota((16, 2 * CZ), 1) // 16
    own = column < NORB
    wanted = jnp.where(own, column + band * NORB, column - NORB + (1 - band) * NORB)
    choose_in = (iota((16, 2 * CZ), 0) == wanted).astype(F32).astype(BF16)
    rows_of = dot(choose_out, panel_ref[...], NT).astype(BF16)
    spread_panel = dot(rows_of, choose_in)
    same = iota((CZ, 2 * CZ), 0) % 16 == iota((CZ, 2 * CZ), 1) % 16
    mix[...] = jnp.where(same, spread_panel, 0.0).astype(BF16)

    for copy in pot_loads:
        copy.wait()
    center = KINETIC * 3.0 * COEFFS[0] - CENTER
    weight[...] = (weight[...] + center) * (1.0 / HALF_WIDTH)
    slope = KINETIC / (SCALE * HALF_WIDTH)

    for g in range(NGROUP):
        scale_sums(0, g)
    for g in range(NGROUP):
        add_projectors(0, g)
    plane_load.wait()
    line_load.wait()
    edge_load.wait()

    def first_chunk(c):
        wait_recv_all(lambda d: halo(0, c, d))
        for o in range(c * CHUNK, (c + 1) * CHUNK):
            base = weight[...].reshape(ROWS, CZ) * start[o].reshape(ROWS, CZ)
            values = slope * applied(0, c, o) + base
            first[o] = values
            keep(1, o, values)
        send_halos(1, c)

    def second_chunk(c):
        wait_recv_all(lambda d: halo(1, c, d))
        for o in range(c * CHUNK, (c + 1) * CHUNK):
            base = weight[...].reshape(ROWS, CZ) * first[o]
            values = 2.0 * (slope * applied(1, c, o) + base) - start[o].reshape(ROWS, CZ)
            filtered[o] = values.astype(BF16).reshape(2, HALF, CZ)
        exchange(c).start()

    first_chunk(0)
    first_chunk(1)
    project(1, 0)
    first_chunk(2)
    first_chunk(3)
    project(1, 1)
    scale_sums(1, 0)
    add_projectors(1, 0)
    second_chunk(0)
    scale_sums(1, 1)
    second_chunk(1)
    add_projectors(1, 1)
    second_chunk(2)
    second_chunk(3)

    for c in range(NCHUNK):
        exchange(c).wait_recv()
    outs = []
    for h in range(2):
        for part in range(6):
            rows = slice(part * 16, (part + 1) * 16)
            cells = jnp.concatenate(
                [filtered[:, h, rows].reshape(CZ, CZ), partner[:, h, rows].reshape(CZ, CZ)], axis=0
            )
            result[:, h, 2 * part : 2 * part + 2] = dot(mix[...], cells).reshape(NORB, 2, 8, CZ)
        copy = pltpu.make_async_copy(result.at[:, h], out_hbm.at[0, :, :, pl.ds(h * 8, 8), :], out_sem.at[h])
        copy.start()
        outs.append(copy)

    for c in range(NCHUNK):
        exchange(c).wait_send()
    for h in range(2):
        for c in range(NCHUNK):
            wait_send_all(lambda d: halo(h, c, d))
        for g in range(NGROUP):
            for kind in range(2):
                wait_send_all(lambda d: table(h, g, kind, d))
    for copy in outs:
        copy.wait()


def shards(orbitals, potential, projectors, entry_atom, entry_block, kb_energy, panel):
    tables = [jnp.asarray(t) for t in stencil_tables()]
    anywhere = pl.BlockSpec(memory_space=pltpu.HBM)
    vmem = pl.BlockSpec(memory_space=pltpu.VMEM)
    dma = pltpu.SemaphoreType.DMA
    return pl.pallas_call(
        kernel,
        out_shape=jax.ShapeDtypeStruct((1, NORB, CX, CY, CZ), F32),
        in_specs=[anywhere, anywhere, anywhere, vmem, vmem, anywhere, vmem] + [anywhere] * 4,
        out_specs=anywhere,
        scratch_shapes=[
            pltpu.VMEM((NORB, 2, CX, 8, CZ), F32),
            pltpu.VMEM((2, NORB, 8, HALF, CZ), BF16),
            pltpu.VMEM((NORB, ROWS, CZ), F32),
            pltpu.VMEM((2, CX, 8, CZ), F32),
            pltpu.VMEM((4 * ENT, CZ), BF16),
            pltpu.VMEM((4, min(128, kb_energy.shape[0])), F32),
            pltpu.VMEM((ROWS, 8 * HALF), BF16),
            pltpu.VMEM((2 * CZ, CZ), BF16),
            pltpu.VMEM((NORB, 2 * CZ, CZ), BF16),
            pltpu.VMEM((NORB, CZ, 2 * CZ), BF16),
            pltpu.VMEM((2, NCHUNK, 2, ROWS, CZ), BF16),
            pltpu.VMEM((2, NCHUNK, 2, ROWS, CZ), BF16),
            pltpu.VMEM((NORB, 2, HALF, CZ), BF16),
            pltpu.VMEM((NORB, 2, HALF, CZ), BF16),
            pltpu.VMEM((NORB, 2, CX, 8, CZ), F32),
            pltpu.VMEM((ENT, ROWS), BF16),
            pltpu.VMEM((ROWS, 2 * ENT), BF16),
            pltpu.VMEM((CZ, 4 * ENT), BF16),
            pltpu.VMEM((8, GROUP, 32, 2 * CZ), BF16),
            pltpu.VMEM((GROUP * 8, 4 * ENT), F32),
            pltpu.VMEM((NORB, 2, ENT, CZ), BF16),
            pltpu.VMEM((2, NGROUP, 8, CZ), F32),
            pltpu.VMEM((2, NGROUP, 6, 8, CZ), F32),
            pltpu.VMEM((2, NGROUP, 8, CZ), F32),
            pltpu.VMEM((2, NGROUP, 6, 8, CZ), F32),
            pltpu.VMEM((CZ, 2 * CZ), BF16),
            dma((2 * NCHUNK + 8,)),
            dma((2, NCHUNK, 6)),
            dma((2, NCHUNK, 6)),
            dma((2, NGROUP, 2, 6)),
            dma((2, NGROUP, 2, 6)),
            dma((NCHUNK,)),
            dma((NCHUNK,)),
            dma((2,)),
        ],
        compiler_params=pltpu.CompilerParams(
            collective_id=0, has_side_effects=True, vmem_limit_bytes=62 * 1024 * 1024
        ),
    )(
        orbitals,
        potential,
        projectors.reshape(-1, projectors.shape[2]),
        entry_atom.reshape(1, -1),
        entry_block.reshape(1, -1),
        kb_energy.T,
        panel,
        *tables,
    )


def solution(mesh):
    in_specs = (
        P("dom", "band", None, None, None),
        P("dom", None, None, None),
        P("dom", None, None),
        P("dom"),
        P("dom"),
        P(),
        P(),
    )
    out_specs = P("dom", "band", None, None, None)
    return jax.shard_map(shards, mesh=mesh, in_specs=in_specs, out_specs=out_specs, check_vma=False)
```

time: 362 us -> 67.1 us (0.19)
  the two profiles are of different devices: /device:TPU:1 before, /device:TPU:12 now
where the time goes in v1:
time: 67.1 us; the launch traced here: 66.9 us
  Pallas kernels  64.8 us (97%)
  local copies, waits for them, and re-layouts  2.06 us (3%)
    pallas_call x1, Pallas kernels, shards(): pl.pallas_call(kernel, out_shape=jax.ShapeDtypeStruct((1, NORB, CX, CY, C...  64.8 us
    unnamed x1, local copies, waits for them, and re-layouts  2.06 us

profile of v1, /device:TPU:12, one launch (start us, length us, event | category | flops | bytes accessed | tf_op | source)
XLA Modules:
  0.0 66.9 jit_solution(6736248366366123567)
XLA Ops:
  0.0 64.8 %shard_map.109 = f32[1,8,12,16,128]{4,3,2,1,0:T(8,128)} custom-call(f32[1,8,12,16,128]{4,3,2,1,0:T(8,128)} %orb_hbm.1, f32[1,12,16,128]{3,2,1,0:T(8,128)} %pot_hbm.1, bf16[1024,128]{1,0:T(8,128)(2,1)} %bitcast.4, s32[1,256]{1,0:T(1,128)} %bitcast.6, s32[1,256]{1,0:T(1,128)} %bitcast.7, f32[4,1024]{1,0:T(4,128)} %bitcast.5, bf16[16,16]{1,0:T(8,128)(2,1)} %panel_ref.1, ...), custom_call_target="tpu_custom_call" | custom-call | tf_op jit(solution)/shard_map/pallas_call | solution.py:458
  64.9 2.1 %copy.13 = f32[1,8,12,16,128]{4,3,2,1,0:T(8,128)} copy(f32[1,8,12,16,128]{4,3,2,1,0:T(8,128)} %shard_map.109) | data formatting | bytes 1572864

commit v2 on v1

--- a/solution.py
+++ b/solution.py
@@ -276,7 +276,7 @@
         if c == 0:
             pack_load.wait()
             pl.semaphore_wait(barrier, partners)
-        send_halos(0, c)
+            send_halos(0, c)
 
     proj_load.wait()
     mask = iota((32, CZ), 0) == iota((32, CZ), 1) // 4
@@ -366,6 +366,7 @@
 
     for g in range(NGROUP):
         project(0, g)
+    send_halos(0, 1)
 
     jj = iota((CZ, 16), 0) // 16 + band * NORB
     choose_out = (iota((CZ, 16), 1) == jj).astype(F32).astype(BF16)
@@ -386,6 +387,8 @@
 
     for g in range(NGROUP):
         scale_sums(0, g)
+    send_halos(0, 2)
+    send_halos(0, 3)
     for g in range(NGROUP):
         add_projectors(0, g)
     plane_load.wait()
@@ -399,7 +402,6 @@
             values = slope * applied(0, c, o) + base
             first[o] = values
             keep(1, o, values)
-        send_halos(1, c)
 
     def second_chunk(c):
         wait_recv_all(lambda d: halo(1, c, d))
@@ -410,15 +412,19 @@
         exchange(c).start()
 
     first_chunk(0)
+    send_halos(1, 0)
     first_chunk(1)
     project(1, 0)
+    send_halos(1, 1)
     first_chunk(2)
     first_chunk(3)
     project(1, 1)
     scale_sums(1, 0)
+    send_halos(1, 2)
+    scale_sums(1, 1)
+    send_halos(1, 3)
     add_projectors(1, 0)
     second_chunk(0)
-    scale_sums(1, 1)
     second_chunk(1)
     add_projectors(1, 1)
     second_chunk(2)

time: 67.1 us -> 56.3 us (0.84)
  the two profiles are of different devices: /device:TPU:12 before, /device:TPU:8 now
where the time goes in v2:
time: 56.3 us; the launch traced here: 56.1 us
  Pallas kernels  54 us (96%)
  local copies, waits for them, and re-layouts  2.06 us (4%)
    pallas_call x1, Pallas kernels, shards(): pl.pallas_call(kernel, out_shape=jax.ShapeDtypeStruct((1, NORB, CX, CY, C...  54 us
    unnamed x1, local copies, waits for them, and re-layouts  2.06 us

profile of v2, /device:TPU:8, one launch (start us, length us, event | category | flops | bytes accessed | tf_op | source)
XLA Modules:
  0.0 56.1 jit_solution(9624054529686767116)
XLA Ops:
  0.0 54.0 %shard_map.109 = f32[1,8,12,16,128]{4,3,2,1,0:T(8,128)} custom-call(f32[1,8,12,16,128]{4,3,2,1,0:T(8,128)} %orb_hbm.1, f32[1,12,16,128]{3,2,1,0:T(8,128)} %pot_hbm.1, bf16[1024,128]{1,0:T(8,128)(2,1)} %bitcast.4, s32[1,256]{1,0:T(1,128)} %bitcast.6, s32[1,256]{1,0:T(1,128)} %bitcast.7, f32[4,1024]{1,0:T(4,128)} %bitcast.5, bf16[16,16]{1,0:T(8,128)(2,1)} %panel_ref.1, ...), custom_call_target="tpu_custom_call" | custom-call | tf_op jit(solution)/shard_map/pallas_call | solution.py:464
  54.0 2.1 %copy.13 = f32[1,8,12,16,128]{4,3,2,1,0:T(8,128)} copy(f32[1,8,12,16,128]{4,3,2,1,0:T(8,128)} %shard_map.109) | data formatting | bytes 1572864

commit v3 on v2

--- a/solution.py
+++ b/solution.py
@@ -33,7 +33,10 @@
 NCHUNK = NORB // CHUNK
 GROUP = 4
 NGROUP = NORB // GROUP
+MID_Y = DOM_Y // 2
+RELAYED = (0, 1) if MID_Y > 1 else ()
 LANE_SLOT = 16
+XPARTS = 1
 SCALE = 64 * 1.0937445
 F32 = jnp.float32
 BF16 = jnp.bfloat16
@@ -104,11 +107,11 @@
 
 def kernel(
     orb_hbm, pot_hbm, proj_hbm, atom_ref, block_ref, energy_hbm, panel_ref, plane_hbm, line_hbm, edge_hbm, pack_hbm,
-    out_hbm,
+    own_hbm, partner_hbm, mix_hbm,
     start, field, first, weight, proj, energy, plane, line, edge, pack,
-    z_out, z_in, filtered, partner, result,
-    pick, spread, slots, picked, inner, additions, table_out, table_in, scaled_out, scaled_in, mix,
-    local_sem, halo_send, halo_recv, table_send, table_recv, band_send, band_recv, out_sem,
+    z_out, z_in, filtered,
+    pick, spread, slots, picked, inner, additions, table_out, table_in, scaled_out, scaled_in, mix, relay_in,
+    local_sem, halo_send, halo_recv, table_send, table_recv, band_send, band_recv, relay_send, relay_recv, out_sem,
 ):
     dom = lax.axis_index("dom")
     band = lax.axis_index("band")
@@ -124,6 +127,40 @@
 
     def toward(d):
         return {"dom": jnp.clip(dom + strides[d], 0, count - 1)}
+
+    def away(offset):
+        return {"dom": jnp.clip(dom + offset * DOM_Z, 0, count - 1)}
+
+    relay_pairs = (
+        (0, (MID_Y - 1, MID_Y)),
+        (MID_Y - 1, (1 - MID_Y, MID_Y)),
+        (MID_Y, (MID_Y - 1, -MID_Y)),
+        (DOM_Y - 1, (1 - MID_Y, -MID_Y)),
+    )
+    routes = {
+        2: (MID_Y - 1, 1 - MID_Y, 0, MID_Y),
+        3: (MID_Y, MID_Y - 1, DOM_Y - 1, -MID_Y),
+    }
+
+    barrier = pltpu.get_barrier_semaphore()
+    partners = jnp.int32(1)
+    for d in range(6):
+        partners = partners + has[d].astype(jnp.int32)
+
+        @pl.when(has[d])
+        def _():
+            pl.semaphore_signal(barrier, inc=1, device_id=toward(d), device_id_type=pl.DeviceIdType.MESH)
+
+    pl.semaphore_signal(barrier, inc=1, device_id={"band": 1 - band}, device_id_type=pl.DeviceIdType.MESH)
+    for place, offsets in relay_pairs if RELAYED else ():
+        partners = partners + jnp.where(at[1] == place, 2, 0)
+
+        @pl.when(at[1] == place)
+        def _():
+            for offset in offsets:
+                pl.semaphore_signal(
+                    barrier, inc=1, device_id=away(offset), device_id_type=pl.DeviceIdType.MESH
+                )
 
     loads = []
 
@@ -152,17 +189,6 @@
     line_load = load(line_hbm, line)
     edge_load = load(edge_hbm, edge)
 
-    barrier = pltpu.get_barrier_semaphore()
-    partners = jnp.int32(1)
-    for d in range(6):
-        partners = partners + has[d].astype(jnp.int32)
-
-        @pl.when(has[d])
-        def _():
-            pl.semaphore_signal(barrier, inc=1, device_id=toward(d), device_id_type=pl.DeviceIdType.MESH)
-
-    pl.semaphore_signal(barrier, inc=1, device_id={"band": 1 - band}, device_id_type=pl.DeviceIdType.MESH)
-
     for h in range(2):
         for d in range(6):
 
@@ -178,8 +204,8 @@
                     field[h, :, 5, :, :] = jnp.zeros((NORB, HALF, CZ), BF16)
                 else:
                     z_in[h, :, d - 4] = jnp.zeros((NCHUNK, ROWS, CZ), BF16)
-                table_in[h, :, d] = jnp.zeros((NGROUP, 8, CZ), F32)
-                scaled_in[h, :, d] = jnp.zeros((NGROUP, 8, CZ), F32)
+                table_in[h, d] = jnp.zeros((NGROUP, 8, CZ), F32)
+                scaled_in[h, d] = jnp.zeros((NGROUP, 8, CZ), F32)
 
     table_out[...] = jnp.zeros(table_out.shape, F32)
 
@@ -207,25 +233,56 @@
             device_id_type=pl.DeviceIdType.MESH,
         )
 
-    def table(h, g, kind, d):
+    def to_relay(h, c, d):
         return pltpu.make_async_remote_copy(
-            src_ref=(table_out, scaled_out)[kind].at[h, g],
-            dst_ref=(table_in, scaled_in)[kind].at[h, g, d],
-            send_sem=table_send.at[h, g, kind, d],
-            recv_sem=table_recv.at[h, g, kind, d],
+            src_ref=field.at[h, pl.ds(c * CHUNK, CHUNK), 3 - d],
+            dst_ref=relay_in.at[h, RELAYED.index(c)],
+            send_sem=halo_send.at[h, c, d],
+            recv_sem=relay_recv.at[h, RELAYED.index(c)],
+            device_id=away(routes[d][1]),
+            device_id_type=pl.DeviceIdType.MESH,
+        )
+
+    def from_relay(h, c, d):
+        return pltpu.make_async_remote_copy(
+            src_ref=relay_in.at[h, RELAYED.index(c)],
+            dst_ref=field.at[h, pl.ds(c * CHUNK, CHUNK), 2 + d],
+            send_sem=relay_send.at[h, RELAYED.index(c)],
+            recv_sem=halo_recv.at[h, c, d],
+            device_id=away(routes[d][3]),
+            device_id_type=pl.DeviceIdType.MESH,
+        )
+
+    def forward(h, c):
+        for d in routes if c in RELAYED else ():
+
+            @pl.when(at[1] == routes[d][2])
+            def _():
+                to_relay(h, c, d).wait_recv()
+                from_relay(h, c, d).start()
+
+    def table(h, gs, kind, d):
+        return pltpu.make_async_remote_copy(
+            src_ref=(table_out, scaled_out)[kind].at[h, pl.ds(gs[0], len(gs))],
+            dst_ref=(table_in, scaled_in)[kind].at[h, d, pl.ds(gs[0], len(gs))],
+            send_sem=table_send.at[h, gs[0], kind, d],
+            recv_sem=table_recv.at[h, gs[0], kind, d],
             device_id=toward(d),
             device_id_type=pl.DeviceIdType.MESH,
         )
 
-    def exchange(c):
+    def exchange(o):
         return pltpu.make_async_remote_copy(
-            src_ref=filtered.at[pl.ds(c * CHUNK, CHUNK)],
-            dst_ref=partner.at[pl.ds(c * CHUNK, CHUNK)],
-            send_sem=band_send.at[c],
-            recv_sem=band_recv.at[c],
+            src_ref=filtered.at[o],
+            dst_ref=partner_hbm.at[o],
+            send_sem=band_send.at[o],
+            recv_sem=band_recv.at[o],
             device_id={"band": 1 - band},
             device_id_type=pl.DeviceIdType.MESH,
         )
+
+    def store(o):
+        return pltpu.make_async_copy(filtered.at[o], own_hbm.at[o], out_sem.at[o])
 
     def start_all(make):
         for d in range(6):
@@ -266,7 +323,18 @@
             ends = part if ends is None else ends + part
         z_out[h, c, 0] = ends[:, :CZ].astype(BF16)
         z_out[h, c, 1] = ends[:, CZ:].astype(BF16)
-        start_all(lambda d: halo(h, c, d))
+        for d in range(6):
+            direct = has[d]
+            if d in routes and c in RELAYED:
+                direct = jnp.logical_and(direct, at[1] != routes[d][0])
+
+                @pl.when(at[1] == routes[d][0])
+                def _():
+                    to_relay(h, c, d).start()
+
+            @pl.when(direct)
+            def _():
+                halo(h, c, d).start()
 
     for c in range(NCHUNK):
         for copy in orb_loads[c]:
@@ -277,6 +345,8 @@
             pack_load.wait()
             pl.semaphore_wait(barrier, partners)
             send_halos(0, c)
+
+    every = tuple(range(NGROUP))
 
     proj_load.wait()
     mask = iota((32, CZ), 0) == iota((32, CZ), 1) // 4
@@ -322,21 +392,26 @@
         high, low = split(inner[...])
         sums = dot(jnp.concatenate([high, low], axis=0), slots[...], NT).reshape(2, GROUP, 8, CZ)
         table_out[h, g, 0:GROUP] = jnp.sum(jnp.sum(sums, axis=0), axis=1)
-        start_all(lambda d: table(h, g, 0, d))
-
-    def scale_sums(h, g):
-        wait_recv_all(lambda d: table(h, g, 0, d))
-        total = table_out[h, g]
-        for d in range(6):
-            total = total + pltpu.roll(table_in[h, g, d], CZ - LANE_SLOT * (d + 1), 1)
-        scaled_out[h, g] = jnp.where(iota((8, CZ), 1) < LANE_SLOT, total * own_energy, 0.0)
-        start_all(lambda d: table(h, g, 1, d))
+
+    def send_sums(h, gs):
+        start_all(lambda d: table(h, gs, 0, d))
+
+    def scale_sums(h, gs):
+        wait_recv_all(lambda d: table(h, gs, 0, d))
+        for g in gs:
+            total = table_out[h, g]
+            for d in range(6):
+                total = total + pltpu.roll(table_in[h, d, g], CZ - LANE_SLOT * (d + 1), 1)
+            scaled_out[h, g] = jnp.where(iota((8, CZ), 1) < LANE_SLOT, total * own_energy, 0.0)
+        start_all(lambda d: table(h, gs, 1, d))
+
+    def wait_scaled(h, gs):
+        wait_recv_all(lambda d: table(h, gs, 1, d))
 
     def add_projectors(h, g):
-        wait_recv_all(lambda d: table(h, g, 1, d))
         scaled = scaled_out[h, g]
         for d in range(6):
-            scaled = scaled + pltpu.roll(scaled_in[h, g, d], LANE_SLOT * (OPPOSITE[d] + 1), 1)
+            scaled = scaled + pltpu.roll(scaled_in[h, d, g], LANE_SLOT * (OPPOSITE[d] + 1), 1)
         high, low = split(scaled)
         entries = dot(jnp.concatenate([high, low], axis=0), slots[...])
         for q in range(8):
@@ -366,7 +441,9 @@
 
     for g in range(NGROUP):
         project(0, g)
+    send_sums(0, every)
     send_halos(0, 1)
+    send_halos(0, 2)
 
     jj = iota((CZ, 16), 0) // 16 + band * NORB
     choose_out = (iota((CZ, 16), 1) == jj).astype(F32).astype(BF16)
@@ -378,6 +455,8 @@
     spread_panel = dot(rows_of, choose_in)
     same = iota((CZ, 2 * CZ), 0) % 16 == iota((CZ, 2 * CZ), 1) % 16
     mix[...] = jnp.where(same, spread_panel, 0.0).astype(BF16)
+    mix_store = pltpu.make_async_copy(mix, mix_hbm, out_sem.at[NORB])
+    mix_store.start()
 
     for copy in pot_loads:
         copy.wait()
@@ -385,11 +464,12 @@
     weight[...] = (weight[...] + center) * (1.0 / HALF_WIDTH)
     slope = KINETIC / (SCALE * HALF_WIDTH)
 
-    for g in range(NGROUP):
-        scale_sums(0, g)
-    send_halos(0, 2)
+    scale_sums(0, every)
+    forward(0, 0)
     send_halos(0, 3)
-    for g in range(NGROUP):
+    forward(0, 1)
+    wait_scaled(0, every)
+    for g in every:
         add_projectors(0, g)
     plane_load.wait()
     line_load.wait()
@@ -409,51 +489,60 @@
             base = weight[...].reshape(ROWS, CZ) * first[o]
             values = 2.0 * (slope * applied(1, c, o) + base) - start[o].reshape(ROWS, CZ)
             filtered[o] = values.astype(BF16).reshape(2, HALF, CZ)
-        exchange(c).start()
+            exchange(o).start()
+            store(o).start()
 
     first_chunk(0)
     send_halos(1, 0)
     first_chunk(1)
     project(1, 0)
+    send_sums(1, (0,))
     send_halos(1, 1)
     first_chunk(2)
     first_chunk(3)
     project(1, 1)
-    scale_sums(1, 0)
+    send_sums(1, (1,))
+    scale_sums(1, (0,))
+    forward(1, 0)
     send_halos(1, 2)
-    scale_sums(1, 1)
+    forward(1, 1)
+    scale_sums(1, (1,))
     send_halos(1, 3)
+    wait_scaled(1, (0,))
     add_projectors(1, 0)
     second_chunk(0)
     second_chunk(1)
+    wait_scaled(1, (1,))
     add_projectors(1, 1)
     second_chunk(2)
     second_chunk(3)
 
-    for c in range(NCHUNK):
-        exchange(c).wait_recv()
-    outs = []
-    for h in range(2):
-        for part in range(6):
-            rows = slice(part * 16, (part + 1) * 16)
-            cells = jnp.concatenate(
-                [filtered[:, h, rows].reshape(CZ, CZ), partner[:, h, rows].reshape(CZ, CZ)], axis=0
-            )
-            result[:, h, 2 * part : 2 * part + 2] = dot(mix[...], cells).reshape(NORB, 2, 8, CZ)
-        copy = pltpu.make_async_copy(result.at[:, h], out_hbm.at[0, :, :, pl.ds(h * 8, 8), :], out_sem.at[h])
-        copy.start()
-        outs.append(copy)
-
-    for c in range(NCHUNK):
-        exchange(c).wait_send()
+    for o in range(NORB):
+        exchange(o).wait_recv()
+    for o in range(NORB):
+        exchange(o).wait_send()
     for h in range(2):
         for c in range(NCHUNK):
             wait_send_all(lambda d: halo(h, c, d))
-        for g in range(NGROUP):
+        for gs in (every,) if h == 0 else tuple((g,) for g in every):
             for kind in range(2):
-                wait_send_all(lambda d: table(h, g, kind, d))
-    for copy in outs:
-        copy.wait()
+                wait_send_all(lambda d: table(h, gs, kind, d))
+        for c in RELAYED:
+            for d in routes:
+
+                @pl.when(at[1] == routes[d][2])
+                def _():
+                    from_relay(h, c, d).wait_send()
+    for o in range(NORB):
+        store(o).wait()
+    mix_store.wait()
+
+
+def rotate(own, partner, mix, out):
+    for part in range(CX // XPARTS // 2):
+        rows = slice(part * 16, (part + 1) * 16)
+        cells = jnp.concatenate([own[:, 0, rows].reshape(CZ, CZ), partner[:, 0, rows].reshape(CZ, CZ)], axis=0)
+        out[0, :, 2 * part : 2 * part + 2] = dot(mix[...], cells).reshape(NORB, 2, 8, CZ)
 
 
 def shards(orbitals, potential, projectors, entry_atom, entry_block, kb_energy, panel):
@@ -461,11 +550,15 @@
     anywhere = pl.BlockSpec(memory_space=pltpu.HBM)
     vmem = pl.BlockSpec(memory_space=pltpu.VMEM)
     dma = pltpu.SemaphoreType.DMA
-    return pl.pallas_call(
+    own, partner, mix = pl.pallas_call(
         kernel,
-        out_shape=jax.ShapeDtypeStruct((1, NORB, CX, CY, CZ), F32),
+        out_shape=(
+            jax.ShapeDtypeStruct((NORB, 2, HALF, CZ), BF16),
+            jax.ShapeDtypeStruct((NORB, 2, HALF, CZ), BF16),
+            jax.ShapeDtypeStruct((CZ, 2 * CZ), BF16),
+        ),
         in_specs=[anywhere, anywhere, anywhere, vmem, vmem, anywhere, vmem] + [anywhere] * 4,
-        out_specs=anywhere,
+        out_specs=(anywhere,) * 3,
         scratch_shapes=[
             pltpu.VMEM((NORB, 2, CX, 8, CZ), F32),
             pltpu.VMEM((2, NORB, 8, HALF, CZ), BF16),
@@ -480,8 +573,6 @@
             pltpu.VMEM((2, NCHUNK, 2, ROWS, CZ), BF16),
             pltpu.VMEM((2, NCHUNK, 2, ROWS, CZ), BF16),
             pltpu.VMEM((NORB, 2, HALF, CZ), BF16),
-            pltpu.VMEM((NORB, 2, HALF, CZ), BF16),
-            pltpu.VMEM((NORB, 2, CX, 8, CZ), F32),
             pltpu.VMEM((ENT, ROWS), BF16),
             pltpu.VMEM((ROWS, 2 * ENT), BF16),
             pltpu.VMEM((CZ, 4 * ENT), BF16),
@@ -489,18 +580,21 @@
             pltpu.VMEM((GROUP * 8, 4 * ENT), F32),
             pltpu.VMEM((NORB, 2, ENT, CZ), BF16),
             pltpu.VMEM((2, NGROUP, 8, CZ), F32),
-            pltpu.VMEM((2, NGROUP, 6, 8, CZ), F32),
+            pltpu.VMEM((2, 6, NGROUP, 8, CZ), F32),
             pltpu.VMEM((2, NGROUP, 8, CZ), F32),
-            pltpu.VMEM((2, NGROUP, 6, 8, CZ), F32),
+            pltpu.VMEM((2, 6, NGROUP, 8, CZ), F32),
             pltpu.VMEM((CZ, 2 * CZ), BF16),
+            pltpu.VMEM((2, max(1, len(RELAYED)), CHUNK, HALF, CZ), BF16),
             dma((2 * NCHUNK + 8,)),
             dma((2, NCHUNK, 6)),
             dma((2, NCHUNK, 6)),
             dma((2, NGROUP, 2, 6)),
             dma((2, NGROUP, 2, 6)),
-            dma((NCHUNK,)),
-            dma((NCHUNK,)),
-            dma((2,)),
+            dma((NORB,)),
+            dma((NORB,)),
+            dma((2, max(1, len(RELAYED)))),
+            dma((2, max(1, len(RELAYED)))),
+            dma((NORB + 1,)),
         ],
         compiler_params=pltpu.CompilerParams(
             collective_id=0, has_side_effects=True, vmem_limit_bytes=62 * 1024 * 1024
@@ -515,6 +609,15 @@
         panel,
         *tables,
     )
+    rows = HALF // XPARTS
+    block = pl.BlockSpec((NORB, 1, rows, CZ), lambda h, x: (0, h, x, 0))
+    return pl.pallas_call(
+        rotate,
+        grid=(2, XPARTS),
+        out_shape=jax.ShapeDtypeStruct((1, NORB, CX, CY, CZ), F32),
+        in_specs=[block, block, pl.BlockSpec((CZ, 2 * CZ), lambda h, x: (0, 0))],
+        out_specs=pl.BlockSpec((1, NORB, CX // XPARTS, 8, CZ), lambda h, x: (0, 0, x, h, 0)),
+    )(own, partner, mix)
 
 
 def solution(mesh):

time: 56.3 us -> 53.4 us (0.948)
  the two profiles are of different devices: /device:TPU:8 before, /device:TPU:12 now
where the time goes in v3:
time: 53.4 us; the launch traced here: 53.2 us
  Pallas kernels  53.2 us (100%)
    pallas_call x1, Pallas kernels, shards(): pl.pallas_call(kernel, out_shape=(jax.ShapeDtypeStruct((NORB, 2, HALF, CZ...  50.9 us
    pallas_call x1, Pallas kernels, shards(): pl.pallas_call(rotate, grid=(2, XPARTS), out_shape=jax.ShapeDtypeStruct((...  2.32 us

profile of v3, /device:TPU:12, one launch (start us, length us, event | category | flops | bytes accessed | tf_op | source)
XLA Modules:
  0.0 53.2 jit_solution(5069100834983921037)
XLA Ops:
  0.0 50.9 %shard_map.109 = (bf16[8,2,96,128]{3,2,1,0:T(8,128)(2,1)}, bf16[8,2,96,128]{3,2,1,0:T(8,128)(2,1)}, bf16[128,256]{1,0:T(8,128)(2,1)}) custom-call(f32[1,8,12,16,128]{4,3,2,1,0:T(8,128)} %orb_hbm.1, f32[1,12,16,128]{3,2,1,0:T(8,128)} %pot_hbm.1, bf16[1024,128]{1,0:T(8,128)(2,1)} %bitcast.4, s32[1,256]{1,0:T(1,128)} %bitcast.6, s32[1,256]{1,0:T(1,128)} %bitcast.7, ...), custom_call_target="tpu_custom_call" | custom-call | tf_op jit(solution)/shard_map/pallas_call | solution.py:553
  50.9 2.3 %shard_map.110 = f32[1,8,12,16,128]{4,3,2,1,0:T(8,128)} custom-call(bf16[8,2,96,128]{3,2,1,0:T(8,128)(2,1)} %get-tuple-element.8.own, bf16[8,2,96,128]{3,2,1,0:T(8,128)(2,1)} %get-tuple-element.9.partner, bf16[128,256]{1,0:T(8,128)(2,1)} %get-tuple-element.10.mix), custom_call_target="tpu_custom_call" | custom-call | tf_op jit(solution)/shard_map/pallas_call | solution.py:614

commit v4 on v3

--- a/solution.py
+++ b/solution.py
@@ -36,7 +36,6 @@
 MID_Y = DOM_Y // 2
 RELAYED = (0, 1) if MID_Y > 1 else ()
 LANE_SLOT = 16
-XPARTS = 1
 SCALE = 64 * 1.0937445
 F32 = jnp.float32
 BF16 = jnp.bfloat16
@@ -107,11 +106,11 @@
 
 def kernel(
     orb_hbm, pot_hbm, proj_hbm, atom_ref, block_ref, energy_hbm, panel_ref, plane_hbm, line_hbm, edge_hbm, pack_hbm,
-    own_hbm, partner_hbm, mix_hbm,
+    out,
     start, field, first, weight, proj, energy, plane, line, edge, pack,
-    z_out, z_in, filtered,
+    z_out, z_in, filtered, partner,
     pick, spread, slots, picked, inner, additions, table_out, table_in, scaled_out, scaled_in, mix, relay_in,
-    local_sem, halo_send, halo_recv, table_send, table_recv, band_send, band_recv, relay_send, relay_recv, out_sem,
+    local_sem, halo_send, halo_recv, table_send, table_recv, band_send, band_recv, relay_send, relay_recv,
 ):
     dom = lax.axis_index("dom")
     band = lax.axis_index("band")
@@ -274,15 +273,12 @@
     def exchange(o):
         return pltpu.make_async_remote_copy(
             src_ref=filtered.at[o],
-            dst_ref=partner_hbm.at[o],
+            dst_ref=partner.at[o],
             send_sem=band_send.at[o],
             recv_sem=band_recv.at[o],
             device_id={"band": 1 - band},
             device_id_type=pl.DeviceIdType.MESH,
         )
-
-    def store(o):
-        return pltpu.make_async_copy(filtered.at[o], own_hbm.at[o], out_sem.at[o])
 
     def start_all(make):
         for d in range(6):
@@ -455,8 +451,6 @@
     spread_panel = dot(rows_of, choose_in)
     same = iota((CZ, 2 * CZ), 0) % 16 == iota((CZ, 2 * CZ), 1) % 16
     mix[...] = jnp.where(same, spread_panel, 0.0).astype(BF16)
-    mix_store = pltpu.make_async_copy(mix, mix_hbm, out_sem.at[NORB])
-    mix_store.start()
 
     for copy in pot_loads:
         copy.wait()
@@ -490,7 +484,6 @@
             values = 2.0 * (slope * applied(1, c, o) + base) - start[o].reshape(ROWS, CZ)
             filtered[o] = values.astype(BF16).reshape(2, HALF, CZ)
             exchange(o).start()
-            store(o).start()
 
     first_chunk(0)
     send_halos(1, 0)
@@ -519,6 +512,14 @@
 
     for o in range(NORB):
         exchange(o).wait_recv()
+    for h in range(2):
+        for part in range(6):
+            rows = slice(part * 16, (part + 1) * 16)
+            cells = jnp.concatenate(
+                [filtered[:, h, rows].reshape(CZ, CZ), partner[:, h, rows].reshape(CZ, CZ)], axis=0
+            )
+            out[0, :, 2 * part : 2 * part + 2, h * 8 : h * 8 + 8] = dot(mix[...], cells).reshape(NORB, 2, 8, CZ)
+
     for o in range(NORB):
         exchange(o).wait_send()
     for h in range(2):
@@ -533,16 +534,6 @@
                 @pl.when(at[1] == routes[d][2])
                 def _():
                     from_relay(h, c, d).wait_send()
-    for o in range(NORB):
-        store(o).wait()
-    mix_store.wait()
-
-
-def rotate(own, partner, mix, out):
-    for part in range(CX // XPARTS // 2):
-        rows = slice(part * 16, (part + 1) * 16)
-        cells = jnp.concatenate([own[:, 0, rows].reshape(CZ, CZ), partner[:, 0, rows].reshape(CZ, CZ)], axis=0)
-        out[0, :, 2 * part : 2 * part + 2] = dot(mix[...], cells).reshape(NORB, 2, 8, CZ)
 
 
 def shards(orbitals, potential, projectors, entry_atom, entry_block, kb_energy, panel):
@@ -550,15 +541,11 @@
     anywhere = pl.BlockSpec(memory_space=pltpu.HBM)
     vmem = pl.BlockSpec(memory_space=pltpu.VMEM)
     dma = pltpu.SemaphoreType.DMA
-    own, partner, mix = pl.pallas_call(
+    return pl.pallas_call(
         kernel,
-        out_shape=(
-            jax.ShapeDtypeStruct((NORB, 2, HALF, CZ), BF16),
-            jax.ShapeDtypeStruct((NORB, 2, HALF, CZ), BF16),
-            jax.ShapeDtypeStruct((CZ, 2 * CZ), BF16),
-        ),
+        out_shape=pltpu.VMEM((1, NORB, CX, CY, CZ), F32),
         in_specs=[anywhere, anywhere, anywhere, vmem, vmem, anywhere, vmem] + [anywhere] * 4,
-        out_specs=(anywhere,) * 3,
+        out_specs=pl.BlockSpec(memory_space=pltpu.VMEM),
         scratch_shapes=[
             pltpu.VMEM((NORB, 2, CX, 8, CZ), F32),
             pltpu.VMEM((2, NORB, 8, HALF, CZ), BF16),
@@ -572,6 +559,7 @@
             pltpu.VMEM((NORB, CZ, 2 * CZ), BF16),
             pltpu.VMEM((2, NCHUNK, 2, ROWS, CZ), BF16),
             pltpu.VMEM((2, NCHUNK, 2, ROWS, CZ), BF16),
+            pltpu.VMEM((NORB, 2, HALF, CZ), BF16),
             pltpu.VMEM((NORB, 2, HALF, CZ), BF16),
             pltpu.VMEM((ENT, ROWS), BF16),
             pltpu.VMEM((ROWS, 2 * ENT), BF16),
@@ -594,7 +582,6 @@
             dma((NORB,)),
             dma((2, max(1, len(RELAYED)))),
             dma((2, max(1, len(RELAYED)))),
-            dma((NORB + 1,)),
         ],
         compiler_params=pltpu.CompilerParams(
             collective_id=0, has_side_effects=True, vmem_limit_bytes=62 * 1024 * 1024
@@ -609,15 +596,6 @@
         panel,
         *tables,
     )
-    rows = HALF // XPARTS
-    block = pl.BlockSpec((NORB, 1, rows, CZ), lambda h, x: (0, h, x, 0))
-    return pl.pallas_call(
-        rotate,
-        grid=(2, XPARTS),
-        out_shape=jax.ShapeDtypeStruct((1, NORB, CX, CY, CZ), F32),
-        in_specs=[block, block, pl.BlockSpec((CZ, 2 * CZ), lambda h, x: (0, 0))],
-        out_specs=pl.BlockSpec((1, NORB, CX // XPARTS, 8, CZ), lambda h, x: (0, 0, x, h, 0)),
-    )(own, partner, mix)
 
 
 def solution(mesh):

time: 53.4 us -> 52.1 us (0.976)
  Pallas kernels: 53.2 us -> 51.1 us
  local copies, waits for them, and re-layouts: 0 us -> 0.88 us
    pallas_call x2 -> x1, Pallas kernels: 53.2 us -> 51.1 us  [shards(): pl.pallas_call(kernel, out_shape=pltpu.VMEM((1, NORB, CX, CY, CZ), F32),...]
    unnamed x0 -> x1, local copies, waits for them, and re-layouts: none -> 0.88 us
where the time goes in v4:
time: 52.1 us; the launch traced here: 52 us
  Pallas kernels  51.1 us (98%)
  local copies, waits for them, and re-layouts  0.88 us (2%)
    pallas_call x1, Pallas kernels, shards(): pl.pallas_call(kernel, out_shape=pltpu.VMEM((1, NORB, CX, CY, CZ), F32),...  51.1 us

profile of v4, /device:TPU:12, one launch (start us, length us, event | category | flops | bytes accessed | tf_op | source)
XLA Modules:
  0.0 52.0 jit_solution(5660485046815064450)
XLA Ops:
  0.0 51.1 %shard_map.109 = f32[1,8,12,16,128]{4,3,2,1,0:T(8,128)S(1)} custom-call(f32[1,8,12,16,128]{4,3,2,1,0:T(8,128)} %orb_hbm.1, f32[1,12,16,128]{3,2,1,0:T(8,128)} %pot_hbm.1, bf16[1024,128]{1,0:T(8,128)(2,1)} %bitcast.4, s32[1,256]{1,0:T(1,128)} %bitcast.6, s32[1,256]{1,0:T(1,128)} %bitcast.7, f32[4,1024]{1,0:T(4,128)} %bitcast.5, bf16[16,16]{1,0:T(8,128)(2,1)} %panel_ref.1, ...), custom_call_target="tpu_custom_call" | custom-call | tf_op jit(solution)/shard_map/pallas_call | solution.py:544
  51.1 0.9 %copy.13 = f32[1,8,12,16,128]{4,3,2,1,0:T(8,128)} copy(f32[1,8,12,16,128]{4,3,2,1,0:T(8,128)S(1)} %shard_map.109) | data formatting | bytes 1572864

commit v5 on v4

--- a/solution.py
+++ b/solution.py
@@ -313,14 +313,15 @@
         field[h, o, 6:8] = low
 
     def send_halos(h, c):
-        ends = None
-        for o in range(c * CHUNK, (c + 1) * CHUNK):
-            part = dot(high_of(h, o), pack[o])
-            ends = part if ends is None else ends + part
-        z_out[h, c, 0] = ends[:, :CZ].astype(BF16)
-        z_out[h, c, 1] = ends[:, CZ:].astype(BF16)
         for d in range(6):
             direct = has[d]
+            if d == 4:
+                ends = None
+                for o in range(c * CHUNK, (c + 1) * CHUNK):
+                    part = dot(high_of(h, o), pack[o])
+                    ends = part if ends is None else ends + part
+                z_out[h, c, 0] = ends[:, :CZ].astype(BF16)
+                z_out[h, c, 1] = ends[:, CZ:].astype(BF16)
             if d in routes and c in RELAYED:
                 direct = jnp.logical_and(direct, at[1] != routes[d][0])
 
@@ -510,15 +511,19 @@
     second_chunk(2)
     second_chunk(3)
 
+    def rotate(first_o, count_o, source, columns, add):
+        for h in range(2):
+            for part in range(6):
+                rows = slice(part * 16, (part + 1) * 16)
+                cells = source[first_o : first_o + count_o, h, rows].reshape(count_o * 16, CZ)
+                value = dot(mix[:, columns : columns + count_o * 16], cells).reshape(NORB, 2, 8, CZ)
+                place = (0, slice(None), slice(2 * part, 2 * part + 2), slice(h * 8, h * 8 + 8))
+                out[place] = out[place] + value if add else value
+
+    rotate(0, NORB, filtered, 0, False)
     for o in range(NORB):
         exchange(o).wait_recv()
-    for h in range(2):
-        for part in range(6):
-            rows = slice(part * 16, (part + 1) * 16)
-            cells = jnp.concatenate(
-                [filtered[:, h, rows].reshape(CZ, CZ), partner[:, h, rows].reshape(CZ, CZ)], axis=0
-            )
-            out[0, :, 2 * part : 2 * part + 2, h * 8 : h * 8 + 8] = dot(mix[...], cells).reshape(NORB, 2, 8, CZ)
+    rotate(0, NORB, partner, CZ, True)
 
     for o in range(NORB):
         exchange(o).wait_send()

time: 52.1 us -> 52.2 us (level)
  no operation moved by 1% of the time
where the time goes in v5:
time: 52.2 us; the launch traced here: 52 us
  Pallas kernels  51.1 us (98%)
  local copies, waits for them, and re-layouts  0.88 us (2%)
    pallas_call x1, Pallas kernels, shards(): pl.pallas_call(kernel, out_shape=pltpu.VMEM((1, NORB, CX, CY, CZ), F32),...  51.1 us

profile of v5, /device:TPU:12, one launch (start us, length us, event | category | flops | bytes accessed | tf_op | source)
XLA Modules:
  0.0 52.0 jit_solution(15730077876009686341)
XLA Ops:
  0.0 51.1 %shard_map.109 = f32[1,8,12,16,128]{4,3,2,1,0:T(8,128)S(1)} custom-call(f32[1,8,12,16,128]{4,3,2,1,0:T(8,128)} %orb_hbm.1, f32[1,12,16,128]{3,2,1,0:T(8,128)} %pot_hbm.1, bf16[1024,128]{1,0:T(8,128)(2,1)} %bitcast.4, s32[1,256]{1,0:T(1,128)} %bitcast.6, s32[1,256]{1,0:T(1,128)} %bitcast.7, f32[4,1024]{1,0:T(4,128)} %bitcast.5, bf16[16,16]{1,0:T(8,128)(2,1)} %panel_ref.1, ...), custom_call_target="tpu_custom_call" | custom-call | tf_op jit(solution)/shard_map/pallas_call | solution.py:549
  51.1 0.9 %copy.13 = f32[1,8,12,16,128]{4,3,2,1,0:T(8,128)} copy(f32[1,8,12,16,128]{4,3,2,1,0:T(8,128)S(1)} %shard_map.109) | data formatting | bytes 1572864
